TPU v7x, 128 devices: a whole 4x4x4 slice. The times are simulated.
128 devices in a mesh: thinker: 4 (over z), seq: 32 (over y, x, core).
Axes of the slice: x: 4, y: 4, z: 4, core: 2. Of those that a mesh axis runs over, the one named last changes fastest.
Arguments:
- queries: bfloat16 [4, 4096, 2048], P('thinker', 'seq'), may hold values from -6 to 6
- keys: bfloat16 [4, 4096, 512], P('thinker', 'seq'), may hold values from -6 to 6
- values: bfloat16 [4, 4096, 512], P('thinker', 'seq'), may hold values from -6 to 6
- forward_out: bfloat16 [4, 4096, 2048], P('thinker', 'seq'), may hold values from -2 to 2
- logsumexp: float32 [4, 16, 4096], P('thinker', None, 'seq'), may hold values from -1 to 16, as said below
- upstream: bfloat16 [128, 128, 2048], P(None, ('thinker', 'seq')), may hold values from -6 to 6
- lengths: int32 [4], replicated, may hold values from 512 to 4096, as said below
- sibling_mask: int32 [4, 3, 32], P('thinker', None, 'seq'), may hold values from 0 to 1, as said below
Outputs:
- query_grad: bfloat16 [4, 4096, 2048], P('thinker', 'seq')
- key_grad: bfloat16 [4, 4096, 512], P('thinker', 'seq')
- value_grad: bfloat16 [4, 4096, 512], P('thinker', 'seq')
Inputs may be any that keep to these rules, and one draw needn't show every extreme that they name: lengths[t] valid positions stand at the start of thinker t's trace; two thinkers have exactly 4096, one exactly 512. sibling_mask[t, r, b] = 1 where query block b of thinker t reads the recent tokens of thinker (t + r + 1) % 4; the two thinkers of length 4096 read each other in the blocks of the last 128 positions. `logsumexp`: rows of positions past a trace's length carry arbitrary values.
All inputs are finite; a program needn't handle non-finite values.
Results may differ from a plain program's by a relative error of at most 0.014.
Values may be sent and summed in bfloat16 or wider, within the bound.
No kernel may reach another device: no remote copies, remote signals or barrier semaphores. Data moves between devices by JAX's collectives and lax.ppermute only.
A program may use at most 128 MiB of HBM per device.

v0:
```python
import math

import jax
import jax.numpy as jnp
from jax import lax
from jax.sharding import PartitionSpec as P

BLOCK = 128


def from_behind(block, axis, distance):
    devices = range(lax.axis_size(axis))
    route = [(i - distance, i) for i in devices if i - distance in devices]
    return lax.ppermute(block, axis, route)


def pair_grads(
    query_heads, upstream_heads, lse_heads, delta_heads, key_rows, value_rows, allowed, factor
):
    count = key_rows.shape[0]
    kv_heads = query_heads.shape[1]
    head_dim = query_heads.shape[3]
    key_heads = key_rows.reshape(count, kv_heads, head_dim)
    value_heads = value_rows.reshape(count, kv_heads, head_dim)
    scores = (
        jnp.einsum("ikgd,jkd->kgij", query_heads, key_heads, preferred_element_type=jnp.float32)
        * factor
    )
    probs = jnp.where(allowed, jnp.exp(scores - lse_heads[..., None]), 0.0)
    dprobs = jnp.einsum(
        "ikgd,jkd->kgij", upstream_heads, value_heads, preferred_element_type=jnp.float32
    )
    dscores = probs * (dprobs - delta_heads[..., None])
    probs_low = probs.astype(jnp.bfloat16)
    dscores_low = dscores.astype(jnp.bfloat16)
    value_part = jnp.einsum(
        "kgij,ikgd->jkd", probs_low, upstream_heads, preferred_element_type=jnp.float32
    )
    key_part = (
        jnp.einsum("kgij,ikgd->jkd", dscores_low, query_heads, preferred_element_type=jnp.float32)
        * factor
    )
    query_part = (
        jnp.einsum("kgij,jkd->ikgd", dscores_low, key_heads, preferred_element_type=jnp.float32)
        * factor
    )
    rows = query_heads.shape[0]
    return (
        query_part.reshape(rows, -1),
        key_part.reshape(count, -1),
        value_part.reshape(count, -1),
    )


def shards(queries, keys, values, forward_out, logsumexp, upstream, lengths, sibling_mask):
    thinkers = lax.axis_size("thinker")
    seq_count = lax.axis_size("seq")
    devices = thinkers * seq_count
    rows = queries.shape[1]
    qwidth = queries.shape[2]
    kwidth = keys.shape[2]
    heads = logsumexp.shape[1]
    head_dim = qwidth // heads
    kv_heads = kwidth // head_dim
    group = heads // kv_heads
    factor = head_dim ** (-0.5)
    thinker = lax.axis_index("thinker")
    shard = lax.axis_index("seq")
    length = rows * seq_count
    per_peer = rows // devices
    arranged = upstream.reshape(devices, per_peer, 1, qwidth)
    arrived = lax.all_to_all(arranged, ("thinker", "seq"), split_axis=0, concat_axis=2, tiled=True)
    grad_out = arrived.reshape(rows, qwidth)
    query_heads = queries[0].reshape(rows, kv_heads, group, head_dim)
    upstream_heads = grad_out.reshape(rows, kv_heads, group, head_dim)
    output_heads = forward_out[0].reshape(rows, kv_heads, group, head_dim)
    delta = jnp.sum(upstream_heads.astype(jnp.float32) * output_heads.astype(jnp.float32), axis=-1)
    delta_heads = jnp.transpose(delta, (1, 2, 0))
    lse_heads = logsumexp[0].reshape(kv_heads, group, rows)
    my_length = lengths[thinker]
    first_query = shard * rows
    query_pos = first_query + jnp.arange(rows, dtype=jnp.int32)
    query_live = query_pos < my_length

    def own_block(key_rows, value_rows, key_start):
        count = key_rows.shape[0]
        key_pos = key_start + jnp.arange(count, dtype=jnp.int32)
        allowed = (
            (key_pos[None, :] <= query_pos[:, None])
            & query_live[:, None]
            & (key_pos[None, :] < my_length)
        )
        return pair_grads(
            query_heads,
            upstream_heads,
            lse_heads,
            delta_heads,
            key_rows,
            value_rows,
            allowed,
            factor,
        )

    initial = (
        jnp.zeros((rows, qwidth), jnp.float32),
        jnp.zeros((length, kwidth), jnp.bfloat16),
        jnp.zeros((length, kwidth), jnp.bfloat16),
    )
    piece_keys = lax.all_gather(keys, "seq", axis=1, tiled=True)[0]
    piece_values = lax.all_gather(values, "seq", axis=1, tiled=True)[0]
    piece_rows = piece_keys.shape[0]
    sub_rows = math.gcd(piece_rows, 512)

    def one_block(position, inner):
        total, key_buffer, value_buffer = inner
        offset = position * sub_rows
        key_rows = lax.dynamic_slice_in_dim(piece_keys, offset, sub_rows, 0)
        value_rows = lax.dynamic_slice_in_dim(piece_values, offset, sub_rows, 0)
        query_part, key_part, value_part = own_block(key_rows, value_rows, offset)
        key_buffer = lax.dynamic_update_slice_in_dim(
            key_buffer, key_part.astype(jnp.bfloat16), offset, 0
        )
        value_buffer = lax.dynamic_update_slice_in_dim(
            value_buffer, value_part.astype(jnp.bfloat16), offset, 0
        )
        return (total + query_part, key_buffer, value_buffer)

    query_total, key_buffer, value_buffer = lax.fori_loop(
        0, piece_rows // sub_rows, one_block, initial
    )
    own_key, own_value = (
        lax.psum_scatter(key_buffer, "seq", scatter_dimension=0, tiled=True).astype(jnp.float32),
        lax.psum_scatter(value_buffer, "seq", scatter_dimension=0, tiled=True).astype(jnp.float32),
    )
    sibling_keys, sibling_values = (
        lax.all_gather(keys, "thinker", axis=0, tiled=True),
        lax.all_gather(values, "thinker", axis=0, tiled=True),
    )
    prior_keys, prior_values = from_behind((sibling_keys, sibling_values), "seq", 1)
    window_keys = jnp.roll(jnp.concatenate([prior_keys, sibling_keys], axis=1), -thinker, axis=0)
    window_values = jnp.roll(
        jnp.concatenate([prior_values, sibling_values], axis=1), -thinker, axis=0
    )
    key_pos = first_query - rows + jnp.arange(2 * rows, dtype=jnp.int32)
    near = (
        (key_pos[None, :] <= query_pos[:, None])
        & (key_pos[None, :] > query_pos[:, None] - rows)
        & (key_pos[None, :] >= 0)
        & query_live[:, None]
    )
    mask_rows = sibling_mask[0]
    key_terms_list = [jnp.zeros((2 * rows, kwidth), jnp.float32)]
    value_terms_list = [jnp.zeros((2 * rows, kwidth), jnp.float32)]
    for offset in range(1, thinkers):
        sibling = (thinker + offset) % thinkers
        visible = jnp.repeat(mask_rows[offset - 1], BLOCK) == 1
        allowed = near & visible[:, None] & (key_pos[None, :] < lengths[sibling])
        extra_query, extra_key, extra_value = pair_grads(
            query_heads,
            upstream_heads,
            lse_heads,
            delta_heads,
            window_keys[offset],
            window_values[offset],
            allowed,
            factor,
        )
        query_total = query_total + extra_query
        key_terms_list.append(extra_key)
        value_terms_list.append(extra_value)
    key_stack = jnp.roll(jnp.stack(key_terms_list), thinker, axis=0)
    value_stack = jnp.roll(jnp.stack(value_terms_list), thinker, axis=0)
    sibling_key, sibling_value = (
        lax.psum_scatter(
            key_stack.astype(jnp.bfloat16), "thinker", scatter_dimension=0, tiled=True
        ).astype(jnp.float32),
        lax.psum_scatter(
            value_stack.astype(jnp.bfloat16), "thinker", scatter_dimension=0, tiled=True
        ).astype(jnp.float32),
    )
    earlier_key, earlier_value = (
        from_behind(sibling_key[0, :rows].astype(jnp.bfloat16), "seq", -1).astype(jnp.float32),
        from_behind(sibling_value[0, :rows].astype(jnp.bfloat16), "seq", -1).astype(jnp.float32),
    )
    key_grad = (own_key + sibling_key[0, rows:] + earlier_key).astype(jnp.bfloat16)[None]
    value_grad = (own_value + sibling_value[0, rows:] + earlier_value).astype(jnp.bfloat16)[None]
    return (query_total.astype(jnp.bfloat16)[None], key_grad, value_grad)


def solution(mesh):
    placed = (
        P("thinker", "seq", None),
        P("thinker", "seq", None),
        P("thinker", "seq", None),
        P("thinker", "seq", None),
        P("thinker", None, "seq"),
        P(None, ("thinker", "seq"), None),
        P(),
        P("thinker", None, "seq"),
    )
    return jax.shard_map(
        shards,
        mesh=mesh,
        in_specs=placed,
        out_specs=(P("thinker", "seq", None), P("thinker", "seq", None), P("thinker", "seq", None)),
        check_vma=False,
    )
```

profile of v0, /device:TPU:0, one launch (start us, length us, event | category | flops | bytes accessed | tf_op | source)
XLA Modules:
  0.0 450.8 jit_solution(13187898375791302462)
XLA Ops:
  15.2 11.2 %all-to-all-start = ((bf16[128,2,1024]{2,1,0:T(2,128)(2,1)}), bf16[128,2,1024]{2,1,0:T(2,128)(2,1)S(1)}, u32[]{:S(2)}, u32[]{:S(2)}) async-start(bf16[128,2,1024]{2,1,0:T(2,128)(2,1)} %reshape.165), calls=%async_computation | async-start | bytes 1048576 | tf_op jit(solution)/shard_map/all_to_all | solution.py:72
  26.5 15.7 %all_gather.15 = bf16[4,128,512]{2,1,0:T(8,128)(2,1)S(1)} all-gather(bf16[1,128,512]{2,1,0:T(8,128)(2,1)S(1)} %copy-done.17), channel_id=1, replica_groups=mesh['thinker'=4,'seq'=32] {'thinker'}, dimensions={0}, use_global_device_ids=true | all-gather | bytes 655360 | tf_op jit(solution)/shard_map/all_gather | solution.py:137
  44.6 12.8 %all_gather.14 = bf16[4,128,512]{2,1,0:T(8,128)(2,1)S(1)} all-gather(bf16[1,128,512]{2,1,0:T(8,128)(2,1)S(1)} %copy-done.18), channel_id=1, replica_groups=mesh['thinker'=4,'seq'=32] {'thinker'}, dimensions={0}, use_global_device_ids=true | all-gather | bytes 655360 | tf_op jit(solution)/shard_map/all_gather | solution.py:136
  57.6 3.7 collective-permute-start
  104.4 3.3 fusion.36
  108.5 14.2 %all-gather.5.cloned.1.call-done = bf16[1,4096,512]{1,2,0:T(8,128)(2,1)} async-done(((bf16[1,128,512]{1,2,0:T(8,128)(2,1)}), bf16[1,4096,512]{1,2,0:T(8,128)(2,1)}) %all-gather.5.cloned.1.call-update) | async-done | bytes 4194320 | tf_op jit(solution)/shard_map/all_gather | solution.py:110
  127.2 147.3 %while.20 = (s32[]{:T(128)}, f32[128,2048]{0,1:T(8,128)}, bf16[4096,512]{1,0:T(8,128)(2,1)}, bf16[4096,512]{1,0:T(8,128)(2,1)}, bf16[4096,512]{0,1:T(8,128)(2,1)...) while((s32[]{:T(128)}, f32[128,2048]{0,1:T(8,128)}, ...), condition=%wide.region_2.3_spmd.clone.clone.clone, body=%wide.region_1.2_spmd.clone.clone.clone.sunk | while | flops 1354434432 | bytes 44792396 | solution.py:128
  132.7 2.8 fusion.147
  139.3 2.6 fusion.148
  151.2 2.8 fusion.147
  157.8 2.6 fusion.148
  169.6 2.8 fusion.147
  176.2 2.6 fusion.148
  188.0 2.8 fusion.147
  194.6 2.6 fusion.148
  206.4 2.8 fusion.147
  213.0 2.6 fusion.148
  224.8 2.8 fusion.147
  243.1 2.8 fusion.147
  249.8 2.6 fusion.148
  261.5 2.8 fusion.147
  287.9 2.7 fusion.69
  290.6 65.7 %reduce-scatter.9.cloned.1.call-done = bf16[128,512]{1,0:T(8,128)(2,1)} async-done(((bf16[4096,512]{1,0:T(8,128)(2,1)}), bf16[128,512]{1,0:T(8,128)(2,1)}) %reduce-scatter.9.cloned.1.call-update) | async-done | bytes 131088 | tf_op jit(solution)/shard_map/reduce_scatter | solution.py:133
  358.0 83.6 %reduce-scatter.5.cloned.1.call-done = bf16[128,512]{1,0:T(8,128)(2,1)} async-done(((bf16[4096,512]{1,0:T(8,128)(2,1)}), bf16[128,512]{1,0:T(8,128)(2,1)}) %reduce-scatter.5.cloned.1.call-update) | async-done | bytes 131088 | tf_op jit(solution)/shard_map/reduce_scatter | solution.py:132
  (285 shorter events, 180.7 us)
Async XLA Ops:
  8.0 18.5 %copy-start.17 = (bf16[1,128,512]{2,1,0:T(8,128)(2,1)S(1)}, bf16[1,128,512]{2,1,0:T(8,128)(2,1)}, u32[]{:S(2)}) copy-start(bf16[1,128,512]{2,1,0:T(8,128)(2,1)} %param.16) | copy-start | bytes 393220
  8.0 100.5 %all-gather.3.cloned.1.call-start = ((), (), s32[]{:S(2)}) async-start(), calls=%async_computation.5 | async-start | bytes 4325376 | tf_op jit(solution)/shard_map/all_gather | solution.py:109
  9.8 113.0 %all-gather.5.cloned.1.call-start = ((), (), s32[]{:S(2)}) async-start(), calls=%async_computation.6 | async-start | bytes 4325376 | tf_op jit(solution)/shard_map/all_gather | solution.py:110
  14.0 30.5 %copy-start.18 = (bf16[1,128,512]{2,1,0:T(8,128)(2,1)S(1)}, bf16[1,128,512]{2,1,0:T(8,128)(2,1)}, u32[]{:S(2)}) copy-start(bf16[1,128,512]{2,1,0:T(8,128)(2,1)} %param.15) | copy-start | bytes 393220
  15.2 46.2 %copy-start.22 = (s32[4]{0:T(128)S(1)}, s32[4]{0:T(128)}, u32[]{:S(2)}) copy-start(s32[4]{0:T(128)} %param.20) | copy-start | bytes 52
  15.2 46.8 %copy-start.23 = (s32[1,3,1]{1,2,0:T(1,128)S(1)}, s32[1,3,1]{1,2,0:T(1,128)}, u32[]{:S(2)}) copy-start(s32[1,3,1]{1,2,0:T(1,128)} %param.21) | copy-start | bytes 40
  15.2 50.7 %copy-start.19 = (bf16[1,128,2048]{2,1,0:T(8,128)(2,1)S(1)}, bf16[1,128,2048]{2,1,0:T(8,128)(2,1)}, u32[]{:S(2)}) copy-start(bf16[1,128,2048]{2,1,0:T(8,128)(2,1)} %param.14) | copy-start | bytes 1572868
  15.2 54.5 %all-to-all-start = ((bf16[128,2,1024]{2,1,0:T(2,128)(2,1)}), bf16[128,2,1024]{2,1,0:T(2,128)(2,1)S(1)}, u32[]{:S(2)}, u32[]{:S(2)}) async-start(bf16[128,2,1024]{2,1,0:T(2,128)(2,1)} %reshape.165), calls=%async_computation | async-start | bytes 1048576 | tf_op jit(solution)/shard_map/all_to_all | solution.py:72
  26.4 255.5 %reduce-scatter.11.cloned.1.call-start = ((), (), s32[]{:S(2)}) async-start(), calls=%async_computation.10 | async-start | bytes 1310720 | tf_op jit(solution)/shard_map/reduce_scatter | solution.py:177
  42.4 30.8 %collective-permute-start.1 = (bf16[4,128,512]{1,2,0:T(8,128)(2,1)S(1)}, bf16[4,128,512]{1,2,0:T(8,128)(2,1)}, u32[]{:S(2)}, u32[]{:S(2)}) collective-permute-start(bf16[4,128,512]{1,2,0:T(8,128)(2,1)S(1)} %copy.162), channel_id=1, source_target_pairs={{0,1},{1,2},{2,3},{3,4},{4,5},{5,6},{6,7},{7,8},{8,9},{9,10},{10,1... | collective-permute-start | bytes 1572872 | tf_op jit(solution)/shard_map/ppermute | solution.py:14
  57.6 15.6 %collective-permute-start = (bf16[4,128,512]{1,2,0:T(8,128)(2,1)S(1)}, bf16[4,128,512]{1,2,0:T(8,128)(2,1)}, u32[]{:S(2)}, u32[]{:S(2)}) collective-permute-start(bf16[4,128,512]{1,2,0:T(8,128)(2,1)S(1)} %copy.158), channel_id=1, source_target_pairs={{0,1},{1,2},{2,3},{3,4},{4,5},{5,6},{6,7},{7,8},{8,9},{9,10},{10,1... | collective-permute-start | bytes 1572872 | tf_op jit(solution)/shard_map/ppermute | solution.py:14
  73.2 3.9 copy-start.24
  107.7 176.6 %reduce-scatter.7.cloned.1.call-start = ((), (), s32[]{:S(2)}) async-start(), calls=%async_computation.8 | async-start | bytes 1310720 | tf_op jit(solution)/shard_map/reduce_scatter | solution.py:174
  108.2 248.1 %reduce-scatter.9.cloned.1.call-start = ((), (), s32[]{:S(2)}) async-start(), calls=%async_computation.9 | async-start | bytes 4325376 | tf_op jit(solution)/shard_map/reduce_scatter | solution.py:133
  274.6 166.9 %reduce-scatter.5.cloned.1.call-start = ((), (), s32[]{:S(2)}) async-start(), calls=%async_computation.7 | async-start | bytes 4325376 | tf_op jit(solution)/shard_map/reduce_scatter | solution.py:132
  277.6 2.7 copy-start.9
  277.6 2.7 copy-start.12
  280.3 6.2 %copy-start.2 = (f32[128,2048]{0,1:T(8,128)S(1)}, f32[128,2048]{0,1:T(8,128)}, u32[]{:S(2)}) copy-start(f32[128,2048]{0,1:T(8,128)} %get-tuple-element.221) | copy-start | bytes 3145732
  280.6 7.2 %copy-start.10 = (f32[128,2048]{1,0:T(8,128)S(1)}, f32[128,2048]{1,0:T(8,128)}, u32[]{:S(2)}) copy-start(f32[128,2048]{1,0:T(8,128)} %copy.174) | copy-start | bytes 3145732
  282.0 5.9 %copy-start.11 = (f32[128,2048]{1,0:T(8,128)S(1)}, f32[128,2048]{1,0:T(8,128)}, u32[]{:S(2)}) copy-start(f32[128,2048]{1,0:T(8,128)} %copy.168) | copy-start | bytes 3145732
  283.0 7.6 %collective-permute-start.3 = (bf16[128,512]{1,0:T(8,128)(2,1)S(1)}, bf16[128,512]{1,0:T(8,128)(2,1)}, u32[]{:S(2)}, u32[]{:S(2)}) collective-permute-start(bf16[128,512]{1,0:T(8,128)(2,1)S(1)} %slice_bitcast_fusion), channel_id=1, source_target_pairs={{1,0},{2,1},{3,2},{4,3},{5,4},{6,5},{7,6},{8,7},{9,8},{10,9},{11,1... | collective-permute-start | bytes 393224 | tf_op jit(solution)/shard_map/ppermute | solution.py:14
  285.2 72.8 %collective-permute-start.2 = (bf16[128,512]{1,0:T(8,128)(2,1)S(1)}, bf16[128,512]{1,0:T(8,128)(2,1)S(1)}, u32[]{:S(2)}, u32[]{:S(2)}) collective-permute-start(bf16[128,512]{1,0:T(8,128)(2,1)S(1)} %slice_bitcast_fusion.2), channel_id=1, source_target_pairs={{1,0},{2,1},{3,2},{4,3},{5,4},{6,5},{7,6},{8,7},{9,8},{10,9},{11,1... | collective-permute-start | bytes 393224 | tf_op jit(solution)/shard_map/ppermute | solution.py:14
  287.9 68.5 %copy-start.20 = (bf16[1,256,512]{2,1,0:T(8,128)(2,1)S(1)}, bf16[1,256,512]{2,1,0:T(8,128)(2,1)}, u32[]{:S(2)}) copy-start(bf16[1,256,512]{2,1,0:T(8,128)(2,1)} %reduce-scatter.11.cloned.1.call-done) | copy-start | bytes 786436
  287.9 153.7 %copy-start.21 = (bf16[1,256,512]{2,1,0:T(8,128)(2,1)S(1)}, bf16[1,256,512]{2,1,0:T(8,128)(2,1)}, u32[]{:S(2)}) copy-start(bf16[1,256,512]{2,1,0:T(8,128)(2,1)} %reduce-scatter.7.cloned.1.call-done) | copy-start | bytes 786436
  (33 other events, 38.8 us)
Sparse Core Ops, SparseCore 0:
  11.6 57.4 all-gather.2
  71.8 50.8 all-gather.4
Sparse Core Ops, SparseCore 1:
  107.7 24.0 reduce-scatter.10
  134.1 23.7 reduce-scatter.6
  274.7 81.6 reduce-scatter.8
  360.0 81.5 reduce-scatter.4
where the time goes:
time: 455 us; the launch traced here: 451 us
  waiting for transfers between devices  165 us (36%)
  matrix products  104 us (23%)
  local copies, waits for them, and re-layouts  83.9 us (18%)
  other arithmetic  30.5 us (7%)
  blocking collectives  28.5 us (6%)
  starting transfers between devices  20.1 us (4%)
  between operations  18.1 us (4%)
    reduce_scatter x1, waiting for transfers between devices, shards(): lax.psum_scatter(key_buffer, 'seq', scatter_dimension=0, tiled=True)  83.6 us
    reduce_scatter x1, waiting for transfers between devices, shards(): lax.psum_scatter(value_buffer, 'seq', scatter_dimension=0, tiled=True)  65.7 us
    dot_general x11, matrix products, pair_grads(): jnp.einsum('kgij,ikgd->jkd', probs_low, upstream_heads, preferred_element...  28.6 us
    dot_general x11, matrix products, pair_grads(): jnp.einsum('kgij,ikgd->jkd', dscores_low, query_heads, preferred_element_...  25.7 us
    dot_general x11, matrix products, pair_grads(): jnp.einsum('ikgd,jkd->kgij', upstream_heads, value_heads, preferred_eleme...  25 us
    dot_general x11, matrix products, pair_grads(): jnp.einsum('ikgd,jkd->kgij', query_heads, key_heads, preferred_element_ty...  19.4 us
    dynamic_update_slice x16, local copies, waits for them, and re-layouts, one_block(): lax.dynamic_update_slice_in_dim(value_buffer, value_part.astype(jnp.bfloa...  18.4 us
    all_gather x1, blocking collectives, shards(): lax.all_gather(values, 'thinker', axis=0, tiled=True)  15.7 us
  transfers between devices with their start and end apart: 11, of which 3 were waited for; matrix products, arithmetic and copies ran while one was open for 44% of the time, Pallas kernels for 0%

commit v1 on v0

v1 whole, which is shorter than its diff:
```python
import jax
import jax.numpy as jnp
from jax import lax
from jax.experimental import pallas as pl
from jax.experimental.pallas import tpu as pltpu
from jax.sharding import Mesh, PartitionSpec as P

B = 128
HD = 128
GROUP = 4
HEADS = 4
ROWS = GROUP * B
STAT = 2 * ROWS
PAY = STAT + 32
FACTOR = HD**-0.5
LOG2E = 1.4426950408889634
SCALE = FACTOR * LOG2E
DEAD = 1e30
F32 = jnp.float32
BF16 = jnp.bfloat16
SEQ = ("y", "x", "c")
VMEM = pl.BlockSpec(memory_space=pltpu.VMEM)
SMEM = pl.BlockSpec(memory_space=pltpu.SMEM)


def nt(a, b):
    return lax.dot_general(a, b, (((1,), (1,)), ((), ())), preferred_element_type=F32)


def nn(a, b):
    return jnp.dot(a, b, preferred_element_type=F32)


def call(kernel, name, outs, n_smem, n_vmem, scratch=(), aliases=None):
    return pl.pallas_call(
        kernel,
        out_shape=outs,
        in_specs=[SMEM] * n_smem + [VMEM] * n_vmem,
        out_specs=jax.tree.map(lambda _: VMEM, outs),
        scratch_shapes=list(scratch),
        input_output_aliases=aliases or {},
        compiler_params=pltpu.CompilerParams(vmem_limit_bytes=48 << 20),
        name=name,
    )


def shape(dims, dtype):
    return jax.ShapeDtypeStruct(dims, dtype)


def split_kv(k_ref, v_ref, out_ref):
    for h in range(HEADS):
        out_ref[h, 0] = k_ref[:, h * HD : (h + 1) * HD]
        out_ref[h, 1] = v_ref[:, h * HD : (h + 1) * HD]


def three(x):
    high = x.astype(BF16)
    rest = x - high.astype(F32)
    mid = rest.astype(BF16)
    low = (rest - mid.astype(F32)).astype(BF16)
    return [high.astype(F32), mid.astype(F32), low.astype(F32)]


def payload(g_ref, o_ref, q_ref, lse_ref, out_ref):
    for c in range(HEADS):
        deltas = []
        for g in range(GROUP):
            cols = slice((c * GROUP + g) * HD, (c * GROUP + g + 1) * HD)
            grad = g_ref[:, cols]
            out_ref[c, g * B : (g + 1) * B, :] = q_ref[:, cols]
            out_ref[c, ROWS + g * B : ROWS + (g + 1) * B, :] = grad
            prod = grad.astype(F32) * o_ref[:, cols].astype(F32)
            deltas.append(jnp.sum(prod.T, axis=0, keepdims=True))
        delta = jnp.concatenate(deltas, axis=0)
        lse = lse_ref[c * GROUP : (c + 1) * GROUP, :]
        rows = three(delta) + three(lse) + [jnp.zeros((8, B), F32)]
        out_ref[c, STAT:PAY, :] = jnp.concatenate(rows, axis=0).astype(BF16)


def load_stats(p_ref, stat_ref, i, start, length):
    raw = p_ref[i, STAT:PAY, :].astype(F32)
    delta = raw[0:4] + raw[4:8] + raw[8:12]
    lse = raw[12:16] + raw[16:20] + raw[20:24]
    pos = start + lax.broadcasted_iota(jnp.int32, (GROUP, B), 1)
    lse = jnp.where(pos < length, lse * LOG2E, DEAD)
    for g in range(GROUP):
        stat_ref[i, 0:1, g * B : (g + 1) * B] = delta[g : g + 1]
        stat_ref[i, 1:2, g * B : (g + 1) * B] = lse[g : g + 1]


def make_own(dist, first, last):
    def kernel(*refs):
        len_ref, p_ref, km_ref, ko_ref = refs[:4]
        refs = refs[4:]
        if not first:
            dq_in = refs[0]
            refs = refs[1:]
        dm_ref, do_ref, dq_out, stat_ref, kt_ref, dk_ref, dv_ref = refs[:7]
        acc_ref = refs[7] if last else dq_out
        thinker = lax.axis_index("z")
        chip = lax.axis_index("x")
        core = lax.axis_index("c")
        length = len_ref[thinker]
        for i in range(4):
            load_stats(p_ref, stat_ref, i, (8 * i + 2 * chip + core) * B, length)
        if first:
            acc_ref[...] = jnp.zeros_like(acc_ref)
        else:
            acc_ref[...] = dq_in[...]
        source = lax.rem(chip + 4 - dist, 4)
        below = (source < chip).astype(jnp.int32)

        def key_tile(m, carry):
            keys = jnp.concatenate([km_ref[m, 0], ko_ref[m, 0]], axis=0)
            vals = jnp.concatenate([km_ref[m, 1], ko_ref[m, 1]], axis=0)
            kt_ref[...] = keys.T
            dk_ref[...] = jnp.zeros_like(dk_ref)
            dv_ref[...] = jnp.zeros_like(dv_ref)

            def query_block(i, inner):
                q = p_ref[i, 0:ROWS, :]
                grad = p_ref[i, ROWS:STAT, :]
                prob = jnp.exp2(nt(keys, q) * SCALE - stat_ref[i, 1:2, :])
                if dist == 0:
                    row = lax.broadcasted_iota(jnp.int32, (2 * B, ROWS), 0)
                    col = lax.broadcasted_iota(jnp.int32, (2 * B, ROWS), 1)
                    half = row // B
                    where_key = jnp.where(core == 0, half, 1 - half) * B + row % B
                    limit = core * B + col % B + jnp.where(i > m, 4 * B, 0)
                    prob = jnp.where(where_key <= limit, prob, 0.0)
                diff = nt(vals, grad) - stat_ref[i, 0:1, :]
                ds = (prob * diff).astype(BF16)
                dv_ref[...] += nn(prob.astype(BF16), grad)
                dk_ref[...] += nn(ds, q)
                acc_ref[i] += nn(kt_ref[...], ds)
                return inner

            lo = m if dist == 0 else m + 1 - below
            lax.fori_loop(lo, 4, query_block, 0)
            dk = (dk_ref[...] * FACTOR).astype(BF16)
            dv = dv_ref[...].astype(BF16)
            dm_ref[m, 0] = dk[:B]
            dm_ref[m, 1] = dv[:B]
            do_ref[m, 0] = dk[B:]
            do_ref[m, 1] = dv[B:]
            return carry

        lax.fori_loop(0, 4, key_tile, 0)
        if last:
            for i in range(4):
                dq_out[i] = (acc_ref[i].T * FACTOR).astype(BF16)

    kv = shape((4, 2, B, HD), BF16)
    dq = shape((4, ROWS, HD), BF16) if last else shape((4, HD, ROWS), F32)
    scratch = [
        pltpu.VMEM((4, 2, ROWS), F32),
        pltpu.VMEM((HD, 2 * B), BF16),
        pltpu.VMEM((2 * B, HD), F32),
        pltpu.VMEM((2 * B, HD), F32),
    ]
    if last:
        scratch.append(pltpu.VMEM((4, HD, ROWS), F32))
    return call(kernel, f"own{dist}", (kv, kv, dq), 1, 3 if first else 4, scratch)


def sibling_kernel(len_ref, mask_ref, p_ref, *refs):
    cur, prev, dcur, dprev = refs[0:3], refs[3:6], refs[6:9], refs[9:12]
    dq_out, stat_ref, acc_ref = refs[12:15]
    thinker = lax.axis_index("z")
    block = lax.axis_index("y") * 8 + lax.axis_index("x") * 2 + lax.axis_index("c")
    length = len_ref[thinker]
    for h in range(HEADS):
        load_stats(p_ref, stat_ref, h, block * B, length)

    def head(h, carry):
        acc_ref[...] = jnp.zeros_like(acc_ref)
        for d in (1, 2, 3):
            other = lax.rem(thinker + 4 - d, 4)
            top = len_ref[other] - (block - 1) * B
            low = jnp.where(block == 0, B, 0)
            live = (mask_ref[3 - d] == 1) & (block * B < length) & (top > 0)
            n = d - 1

            @pl.when(live)
            def _():
                keys = jnp.concatenate([prev[n][h, 0], cur[n][h, 0]], axis=0)
                vals = jnp.concatenate([prev[n][h, 1], cur[n][h, 1]], axis=0)
                q = p_ref[h, 0:ROWS, :]
                grad = p_ref[h, ROWS:STAT, :]
                row = lax.broadcasted_iota(jnp.int32, (2 * B, ROWS), 0)
                col = lax.broadcasted_iota(jnp.int32, (1, ROWS), 1) % B
                lower = jnp.maximum(col, low - 1)
                upper = jnp.minimum(col + B, top - 1)
                prob = jnp.exp2(nt(keys, q) * SCALE - stat_ref[h, 1:2, :])
                prob = jnp.where((row > lower) & (row <= upper), prob, 0.0)
                diff = nt(vals, grad) - stat_ref[h, 0:1, :]
                ds = (prob * diff).astype(BF16)
                dv = nn(prob.astype(BF16), grad).astype(BF16)
                dk = (nn(ds, q) * FACTOR).astype(BF16)
                acc_ref[...] += nn(keys.T, ds)
                dprev[n][h, 0] = dk[:B]
                dprev[n][h, 1] = dv[:B]
                dcur[n][h, 0] = dk[B:]
                dcur[n][h, 1] = dv[B:]

            @pl.when(jnp.logical_not(live))
            def _():
                dprev[n][h] = jnp.zeros((2, B, HD), BF16)
                dcur[n][h] = jnp.zeros((2, B, HD), BF16)

        dq_out[h] = acc_ref[...].T * FACTOR
        return carry

    lax.fori_loop(0, HEADS, head, 0)


def finish(dq_ref, sq_ref, kv_ref, s1_ref, s2_ref, s3_ref, q_out, k_out, v_out):
    for c in range(HEADS):
        for g in range(GROUP):
            rows = slice(g * B, (g + 1) * B)
            cols = slice((c * GROUP + g) * HD, (c * GROUP + g + 1) * HD)
            q_out[:, cols] = (dq_ref[c, rows, :].astype(F32) + sq_ref[c, rows, :]).astype(BF16)
        cols = slice(c * HD, (c + 1) * HD)
        for n, out in ((0, k_out), (1, v_out)):
            total = kv_ref[c, n].astype(F32) + s1_ref[c, n].astype(F32)
            total = total + s2_ref[c, n].astype(F32) + s3_ref[c, n].astype(F32)
            out[:, cols] = total.astype(BF16)


def ring(x, axis, step, count):
    return lax.ppermute(x, axis, [(j, (j + step) % count) for j in range(count)])


def shards(queries, keys, values, forward_out, logsumexp, upstream, lengths, sibling_mask):
    kv = shape((4, 2, B, HD), BF16)
    kv_pos = call(split_kv, "split_kv", kv, 0, 2)(keys[0], values[0])
    cur = [ring(kv_pos, "z", d, 4) for d in (1, 2, 3)]
    kv_own = lax.all_to_all(kv_pos, "y", 0, 0, tiled=True)
    near = {0: kv_own}
    for d in (1, 2, 3):
        near[d] = ring(kv_own, "x", d, 4)
    arrived = lax.all_to_all(
        upstream.reshape(128, 1, 1, 2048), ("z", "y", "x", "c"), split_axis=0, concat_axis=2, tiled=True
    )
    grad = arrived.reshape(B, 2048)
    far = {d: ring(near[d], "c", 1, 2) for d in range(4)}
    prev = [ring(k, SEQ, 1, 32) for k in cur]
    pay = call(payload, "payload", shape((4, PAY, HD), BF16), 0, 4)(
        grad, forward_out[0], queries[0], logsumexp[0]
    )
    pay_head = lax.all_to_all(pay, "y", 0, 0, tiled=True)
    part = {}
    mine, other, dq = make_own(2, True, False)(lengths, pay_head, near[2], far[2])
    part[2] = (mine, other)
    mine, other, dq = make_own(1, False, False)(lengths, pay_head, near[1], far[1], dq)
    part[1] = (mine, other)
    mine, other, dq = make_own(3, False, False)(lengths, pay_head, near[3], far[3], dq)
    part[3] = (mine, other)
    sib = call(
        sibling_kernel,
        "sibling",
        tuple([kv] * 6 + [shape((4, ROWS, HD), F32)]),
        2,
        7,
        [pltpu.VMEM((4, 2, ROWS), F32), pltpu.VMEM((HD, ROWS), F32)],
    )(lengths, sibling_mask.reshape(3), pay, *cur, *prev)
    mine, other, dq = make_own(0, False, True)(lengths, pay_head, near[0], far[0], dq)
    part[0] = (mine, other)
    back = {}
    for d in (2, 1, 3, 0):
        mine, other = part[d]
        both = mine.astype(F32) + ring(other, "c", 1, 2).astype(F32)
        back[d] = ring(both.astype(BF16), "x", -d, 4) if d else both
    own = back[0]
    for d in (1, 2, 3):
        own = own + back[d].astype(F32)
    dq_pos = lax.all_to_all(dq, "y", 0, 0, tiled=True)
    own_pos = lax.all_to_all(own.astype(BF16), "y", 0, 0, tiled=True)
    sums = []
    for d in (1, 2, 3):
        late = ring(sib[2 + d], SEQ, -1, 32).astype(F32)
        sums.append(ring((sib[d - 1].astype(F32) + late).astype(BF16), "z", -d, 4))
    row = shape((B, 512), BF16)
    out = call(finish, "finish", (shape((B, 2048), BF16), row, row), 0, 6)(
        dq_pos, sib[6], own_pos, *sums
    )
    return tuple(o[None] for o in out)


def solution(mesh):
    grid = Mesh(mesh.devices.reshape(4, 4, 4, 2), ("z",) + SEQ)
    rows = P("z", SEQ, None)
    return jax.shard_map(
        shards,
        mesh=grid,
        in_specs=(
            rows,
            rows,
            rows,
            rows,
            P("z", None, SEQ),
            P(None, ("z",) + SEQ, None),
            P(),
            P("z", None, SEQ),
        ),
        out_specs=(rows, rows, rows),
        check_vma=False,
    )
```

time: 455 us -> 143 us (0.31)
  waiting for transfers between devices: 165 us -> 46.7 us
  matrix products: 104 us -> 0 us
  local copies, waits for them, and re-layouts: 83.9 us -> 8.06 us
  Pallas kernels: 0 us -> 30.8 us
  blocking collectives: 28.5 us -> 0 us
  starting transfers between devices: 20.1 us -> 44.6 us
  other arithmetic: 30.5 us -> 9.25 us
  between operations: 18.1 us -> 0.9 us
    reduce_scatter x4 -> x0, waiting for transfers between devices: 149 us -> none  [the longest x1 83.6 us: shards(): lax.psum_scatter(key_buffer, 'seq', scatter_dimension=0, tiled=True)]
    dot_general x55 -> x0, matrix products: 104 us -> none  [the longest x11 28.6 us: pair_grads(): jnp.einsum('kgij,ikgd->jkd', probs_low, upstream_heads, preferred_element...]
    pallas_call x0 -> x8, Pallas kernels: none -> 30.8 us  [the longest x1 7.64 us: shards(): call(sibling_kernel, 'sibling', tuple([kv] * 6 + [shape((4, ROWS, HD), F3...]
    all_gather x2 -> x0, blocking collectives: 28.5 us -> none  [the longest x1 15.7 us: shards(): lax.all_gather(values, 'thinker', axis=0, tiled=True)]
    ppermute x4 -> x26, waiting for transfers between devices: 0.01 us -> 27.3 us  [ring(): lax.ppermute(x, axis, [(j, (j + step) % count) for j in range(count)])]
    dynamic_update_slice x24 -> x0, local copies, waits for them, and re-layouts: 20.1 us -> none  [the longest x16 18.4 us: one_block(): lax.dynamic_update_slice_in_dim(value_buffer, value_part.astype(jnp.bfloa...]
    all_to_all x1 -> x5, waiting for transfers between devices: 0.01 us -> 19.4 us  [the longest x1 12.7 us: shards(): lax.all_to_all(upstream.reshape(128, 1, 1, 2048), ('z', 'y', 'x', 'c'), s...]
    dynamic_slice x17 -> x0, local copies, waits for them, and re-layouts: 18 us -> none  [the longest x8 8.69 us: one_block(): key_rows = lax.dynamic_slice_in_dim(piece_keys, offset, sub_rows, 0)]
  transfers between devices with their start and end apart: 11 -> 31, of which waited for: 3 -> 12; matrix products, arithmetic and copies ran while one was open for 44% -> 6% of each run, Pallas kernels for 0% -> 21%
where the time goes in v1:
time: 143 us; the launch traced here: 140 us
  waiting for transfers between devices  46.7 us (33%)
  starting transfers between devices  44.6 us (31%)
  Pallas kernels  30.8 us (22%)
  other arithmetic  9.25 us (6%)
  local copies, waits for them, and re-layouts  8.06 us (6%)
    ppermute x26, waiting for transfers between devices, ring(): lax.ppermute(x, axis, [(j, (j + step) % count) for j in range(count)])  27.3 us
    ppermute x26, starting transfers between devices, ring(): lax.ppermute(x, axis, [(j, (j + step) % count) for j in range(count)])  19.5 us
    all_to_all x1, waiting for transfers between devices, shards(): lax.all_to_all(upstream.reshape(128, 1, 1, 2048), ('z', 'y', 'x', 'c'), s...  12.7 us
    all_to_all x1, starting transfers between devices, shards(): lax.all_to_all(upstream.reshape(128, 1, 1, 2048), ('z', 'y', 'x', 'c'), s...  11.2 us
    pallas_call x1, Pallas kernels, shards(): call(sibling_kernel, 'sibling', tuple([kv] * 6 + [shape((4, ROWS, HD), F3...  7.64 us
    unnamed x37, local copies, waits for them, and re-layouts  7.55 us
    pallas_call x1, Pallas kernels, shards(): make_own(0, False, True)(lengths, pay_head, near[0], far[0], dq)  7.51 us
    pallas_call x1, Pallas kernels, shards(): make_own(3, False, False)(lengths, pay_head, near[3], far[3], dq)  4.32 us
  transfers between devices with their start and end apart: 31, of which 12 were waited for; matrix products, arithmetic and copies ran while one was open for 6% of the time, Pallas kernels for 21%

profile of v1, /device:TPU:0, one launch (start us, length us, event | category | flops | bytes accessed | tf_op | source)
XLA Modules:
  0.0 140.4 jit_solution(12174333594380117894)
XLA Ops:
  1.1 2.0 %reduce = bf16[128,2048]{1,0:T(8,128)(2,1)S(1)} reduce(bf16[128,1,1,2048]{3,0,2,1:T(8,128)(2,1)} %bitcast.20, bf16[]{:T(256)} %broadcast), dimensions={1,2}, to_apply=%copy.11.reduce_sub_computation | reduce | bytes 1048578 | tf_op jit(solution)/shard_map/reshape | solution.py:244
  4.4 11.2 %all-to-all-start = ((bf16[128,2,1024]{2,1,0:T(2,128)(2,1)}), bf16[128,2,1024]{2,1,0:T(2,128)(2,1)S(1)}, u32[]{:S(2)}, u32[]{:S(2)}) async-start(bf16[128,2,1024]{2,1,0:T(2,128)(2,1)} %reshape.22), calls=%async_computation | async-start | bytes 1048576 | tf_op jit(solution)/shard_map/all_to_all | solution.py:243
  16.3 12.7 %all-to-all-done = bf16[128,2,1024]{2,1,0:T(2,128)(2,1)S(1)} async-done(((bf16[128,2,1024]{2,1,0:T(2,128)(2,1)}), bf16[128,2,1024]{2,1,0:T(2,128)(2,1)S(1)}, u32[]{:S(2)}, u32[]{:S(2)}) %all-to-all-start) | async-done | bytes 524320 | tf_op jit(solution)/shard_map/all_to_all | solution.py:243
  29.0 3.4 %all-to-all-start.2 = ((bf16[4,2,128,128]{3,2,1,0:T(8,128)(2,1)}), bf16[4,2,128,128]{3,2,1,0:T(8,128)(2,1)S(1)}, u32[]{:S(2)}, u32[]{:S(2)}) async-start(bf16[4,2,128,128]{3,2,1,0:T(8,128)(2,1)} %split_kv.1), calls=%async_computation.2 | async-start | bytes 524288 | tf_op jit(solution)/shard_map/all_to_all | solution.py:239
  35.6 3.5 %all-to-all-done.2.refs_2_ = bf16[4,2,128,128]{3,2,1,0:T(8,128)(2,1)S(1)} async-done(((bf16[4,2,128,128]{3,2,1,0:T(8,128)(2,1)}), bf16[4,2,128,128]{3,2,1,0:T(8,128)(2,1)S(1)}, u32[]{:S(2)}, u32[]{:S(2)}) %all-to-all-start.2) | async-done | bytes 262176 | tf_op jit(solution)/shard_map/all_to_all | solution.py:239
  39.1 3.5 %all-to-all-start.1 = ((bf16[4,1056,128]{2,1,0:T(8,128)(2,1)}), bf16[4,1056,128]{2,1,0:T(8,128)(2,1)S(1)}, u32[]{:S(2)}, u32[]{:S(2)}) async-start(bf16[4,1056,128]{2,1,0:T(8,128)(2,1)} %payload.1.p_ref), calls=%async_computation.1 | async-start | bytes 2162688 | tf_op jit(solution)/shard_map/all_to_all | solution.py:252
  44.7 1.8 %collective-permute-start.9 = (bf16[4,2,128,128]{3,2,1,0:T(8,128)(2,1)}, bf16[4,2,128,128]{3,2,1,0:T(8,128)(2,1)S(1)}, u32[]{:S(2)}, u32[]{:S(2)}) collective-permute-start(bf16[4,2,128,128]{3,2,1,0:T(8,128)(2,1)} %split_kv.1), channel_id=1, source_target_pairs={{0,96},{32,0},{64,32},{96,64},{1,97},{33,1},{65,33},{97,65},{2,98}... | collective-permute-start | bytes 786440 | tf_op jit(solution)/shard_map/ppermute | solution.py:232
  48.4 7.9 %collective-permute-done.7.refs_0_ = bf16[4,2,128,128]{3,2,1,0:T(8,128)(2,1)S(1)} collective-permute-done((bf16[4,2,128,128]{3,2,1,0:T(8,128)(2,1)}, bf16[4,2,128,128]{3,2,1,0:T(8,128)(2,1)S(1)}, u32[]{:S(2)}, u32[]{:S(2)}) %collective-permute-start.7) | collective-permute-done | bytes 262176 | tf_op jit(solution)/shard_map/ppermute | solution.py:232
  60.0 2.7 %collective-permute-done.1.refs_2_ = bf16[4,2,128,128]{3,2,1,0:T(8,128)(2,1)S(1)} collective-permute-done((bf16[4,2,128,128]{3,2,1,0:T(8,128)(2,1)S(1)}, bf16[4,2,128,128]{3,2,1,0:T(8,128)(2,1)S(1)}, u32[]{:S(2)}, u32[]{:S(2)}) %collective-permute-start.1) | collective-permute-done | bytes 262176 | tf_op jit(solution)/shard_map/ppermute | solution.py:232
  62.7 4.6 %collective-permute-done.10.refs_3_ = bf16[4,2,128,128]{3,2,1,0:T(8,128)(2,1)S(1)} collective-permute-done((bf16[4,2,128,128]{3,2,1,0:T(8,128)(2,1)S(1)}, bf16[4,2,128,128]{3,2,1,0:T(8,128)(2,1)S(1)}, u32[]{:S(2)}, u32[]{:S(2)}) %collective-permute-start.10) | collective-permute-done | bytes 262176 | tf_op jit(solution)/shard_map/ppermute | solution.py:232
  67.3 2.8 %collective-permute-done.11.refs_4_ = bf16[4,2,128,128]{3,2,1,0:T(8,128)(2,1)S(1)} collective-permute-done((bf16[4,2,128,128]{3,2,1,0:T(8,128)(2,1)S(1)}, bf16[4,2,128,128]{3,2,1,0:T(8,128)(2,1)S(1)}, u32[]{:S(2)}, u32[]{:S(2)}) %collective-permute-start.11) | collective-permute-done | bytes 262176 | tf_op jit(solution)/shard_map/ppermute | solution.py:232
  70.1 2.8 %collective-permute-done.12.refs_5_ = bf16[4,2,128,128]{3,2,1,0:T(8,128)(2,1)S(1)} collective-permute-done((bf16[4,2,128,128]{3,2,1,0:T(8,128)(2,1)S(1)}, bf16[4,2,128,128]{3,2,1,0:T(8,128)(2,1)S(1)}, u32[]{:S(2)}, u32[]{:S(2)}) %collective-permute-start.12) | collective-permute-done | bytes 262176 | tf_op jit(solution)/shard_map/ppermute | solution.py:232
  72.9 7.6 %sibling.1 = (bf16[4,2,128,128]{3,2,1,0:T(8,128)(2,1)S(1)}, bf16[4,2,128,128]{3,2,1,0:T(8,128)(2,1)S(1)}, bf16[4,2,128,128]{3,2,1,0:T(8,128)(2,1)S(1)}, bf16[4,2...) custom-call(s32[4]{0:T(128)S(1)} %copy-done.10, ...), custom_call_target="tpu_custom_call" | custom-call | tf_op jit(solution)/shard_map/sibling/pallas_call | solution.py:260
  85.8 3.8 %own2.1 = (bf16[4,2,128,128]{3,2,1,0:T(8,128)(2,1)S(1)}, bf16[4,2,128,128]{3,2,1,0:T(8,128)(2,1)S(1)}, f32[4,128,512]{2,1,0:T(8,128)S(1)}) custom-call(s32[4]{0:T(128)S(1)} %copy-done.10, bf16[4,1056,128]{2,1,0:T(8,128)(2,1)S(1)} %all-to-all-done.1.refs_1_, bf16[4,2,128,128]{3,2,1,0:T(8,128)(2,1)S(1)} %copy-done.5, bf16[4,2,128,128]{3,2,1,0:T(8,128)(2,1)S(1)} %copy-done.7), custom_call_target="tpu_custom_call" | custom-call | tf_op jit(solution)/shard_map/own2/pallas_call | solution.py:254
  89.7 4.2 %own1.1 = (bf16[4,2,128,128]{3,2,1,0:T(8,128)(2,1)S(1)}, bf16[4,2,128,128]{3,2,1,0:T(8,128)(2,1)S(1)}, f32[4,128,512]{2,1,0:T(8,128)S(1)}) custom-call(s32[4]{0:T(128)S(1)} %copy-done.10, bf16[4,1056,128]{2,1,0:T(8,128)(2,1)S(1)} %all-to-all-done.1.refs_1_, bf16[4,2,128,128]{3,2,1,0:T(8,128)(2,1)S(1)} %collective-permute-done.3.refs_2_, ...), custom_call_target="tpu_custom_call" | custom-call | tf_op jit(solution)/shard_map/own1/pallas_call | solution.py:256
  94.0 4.3 %own3.1 = (bf16[4,2,128,128]{3,2,1,0:T(8,128)(2,1)S(1)}, bf16[4,2,128,128]{3,2,1,0:T(8,128)(2,1)S(1)}, f32[4,128,512]{2,1,0:T(8,128)S(1)}) custom-call(s32[4]{0:T(128)S(1)} %copy-done.10, bf16[4,1056,128]{2,1,0:T(8,128)(2,1)S(1)} %all-to-all-done.1.refs_1_, bf16[4,2,128,128]{3,2,1,0:T(8,128)(2,1)S(1)} %collective-permute-done.1.refs_2_, ...), custom_call_target="tpu_custom_call" | custom-call | tf_op jit(solution)/shard_map/own3/pallas_call | solution.py:258
  101.2 7.5 %own0.1 = (bf16[4,2,128,128]{3,2,1,0:T(8,128)(2,1)S(1)}, bf16[4,2,128,128]{3,2,1,0:T(8,128)(2,1)}, bf16[4,512,128]{2,1,0:T(8,128)(2,1)}) custom-call(s32[4]{0:T(128)S(1)} %copy-done.10, bf16[4,1056,128]{2,1,0:T(8,128)(2,1)S(1)} %all-to-all-done.1.refs_1_, bf16[4,2,128,128]{3,2,1,0:T(8,128)(2,1)S(1)} %all-to-all-done.2.refs_2_, ...), custom_call_target="tpu_custom_call" | custom-call | tf_op jit(solution)/shard_map/own0/pallas_call | solution.py:268
  116.0 3.5 %all-to-all-start.3 = ((bf16[4,512,128]{2,1,0:T(8,128)(2,1)}), bf16[4,512,128]{2,1,0:T(8,128)(2,1)S(1)}, u32[]{:S(2)}, u32[]{:S(2)}) async-start(bf16[4,512,128]{2,1,0:T(8,128)(2,1)} %get-tuple-element.28), calls=%async_computation.3 | async-start | bytes 1048576 | tf_op jit(solution)/shard_map/all_to_all | solution.py:278
  120.6 2.7 %collective-permute-start.23 = (bf16[4,2,128,128]{3,2,1,0:T(8,128)(2,1)}, bf16[4,2,128,128]{3,2,1,0:T(8,128)(2,1)S(1)}, u32[]{:S(2)}, u32[]{:S(2)}) collective-permute-start(bf16[4,2,128,128]{3,2,1,0:T(8,128)(2,1)} %add_convert_fusion.1), channel_id=1, source_target_pairs={{0,64},{32,96},{64,0},{96,32},{1,65},{33,97},{65,1},{97,33},{2,66}... | collective-permute-start | bytes 786440 | tf_op jit(solution)/shard_map/ppermute | solution.py:232
  124.8 2.2 %collective-permute-start.21 = (bf16[4,2,128,128]{3,2,1,0:T(8,128)(2,1)S(1)}, bf16[4,2,128,128]{3,2,1,0:T(8,128)(2,1)S(1)}, u32[]{:S(2)}, u32[]{:S(2)}) collective-permute-start(bf16[4,2,128,128]{3,2,1,0:T(8,128)(2,1)S(1)} %add_convert_fusion.2), channel_id=1, source_target_pairs={{0,96},{32,0},{64,32},{96,64},{1,97},{33,1},{65,33},{97,65},{2,98}... | collective-permute-start | bytes 786440 | tf_op jit(solution)/shard_map/ppermute | solution.py:232
  127.0 2.1 %add_convert_fusion.3 = bf16[4,2,128,128]{3,2,1,0:T(8,128)(2,1)} fusion(bf16[4,2,128,128]{3,2,1,0:T(8,128)(2,1)} %collective-permute-done.19, bf16[4,2,128,128]{3,2,1,0:T(8,128)(2,1)} %collective-permute-done.17, bf16[4,2,128,128]{3,2,1,0:T(8,128)(2,1)} %collective-permute-done.15, bf16[4,2,128,128]{3,2,1,0:T(8,128)(2,1)} %collective-permute-done.13, ...), kind=kLoop, calls=%fused_computation.4 | loop fusion | flops 1310720 | bytes 1572864 | tf_op jit(solution)/shard_map/convert_element_type | solution.py:279
  129.1 3.6 %all-to-all-start.4 = ((bf16[4,2,128,128]{3,2,1,0:T(8,128)(2,1)}), bf16[4,2,128,128]{3,2,1,0:T(8,128)(2,1)S(1)}, u32[]{:S(2)}, u32[]{:S(2)}) async-start(bf16[4,2,128,128]{3,2,1,0:T(8,128)(2,1)} %add_convert_fusion.3), calls=%async_computation.4 | async-start | bytes 524288 | tf_op jit(solution)/shard_map/all_to_all | solution.py:279
  132.6 1.9 %collective-permute-done.25.s3_ref = bf16[4,2,128,128]{3,2,1,0:T(8,128)(2,1)S(1)} collective-permute-done((bf16[4,2,128,128]{3,2,1,0:T(8,128)(2,1)}, bf16[4,2,128,128]{3,2,1,0:T(8,128)(2,1)S(1)}, u32[]{:S(2)}, u32[]{:S(2)}) %collective-permute-start.25) | collective-permute-done | bytes 262176 | tf_op jit(solution)/shard_map/ppermute | solution.py:232
  136.2 3.1 %all-to-all-done.4.kv_ref = bf16[4,2,128,128]{3,2,1,0:T(8,128)(2,1)S(1)} async-done(((bf16[4,2,128,128]{3,2,1,0:T(8,128)(2,1)}), bf16[4,2,128,128]{3,2,1,0:T(8,128)(2,1)S(1)}, u32[]{:S(2)}, u32[]{:S(2)}) %all-to-all-start.4) | async-done | bytes 262176 | tf_op jit(solution)/shard_map/all_to_all | solution.py:279
  (92 shorter events, 34.0 us)
Async XLA Ops:
  4.4 24.7 %all-to-all-start = ((bf16[128,2,1024]{2,1,0:T(2,128)(2,1)}), bf16[128,2,1024]{2,1,0:T(2,128)(2,1)S(1)}, u32[]{:S(2)}, u32[]{:S(2)}) async-start(bf16[128,2,1024]{2,1,0:T(2,128)(2,1)} %reshape.22), calls=%async_computation | async-start | bytes 1048576 | tf_op jit(solution)/shard_map/all_to_all | solution.py:243
  39.1 44.8 %all-to-all-start.1 = ((bf16[4,1056,128]{2,1,0:T(8,128)(2,1)}), bf16[4,1056,128]{2,1,0:T(8,128)(2,1)S(1)}, u32[]{:S(2)}, u32[]{:S(2)}) async-start(bf16[4,1056,128]{2,1,0:T(8,128)(2,1)} %payload.1.p_ref), calls=%async_computation.1 | async-start | bytes 2162688 | tf_op jit(solution)/shard_map/all_to_all | solution.py:252
  42.6 13.7 %collective-permute-start.7 = (bf16[4,2,128,128]{3,2,1,0:T(8,128)(2,1)}, bf16[4,2,128,128]{3,2,1,0:T(8,128)(2,1)S(1)}, u32[]{:S(2)}, u32[]{:S(2)}) collective-permute-start(bf16[4,2,128,128]{3,2,1,0:T(8,128)(2,1)} %split_kv.1), channel_id=1, source_target_pairs={{0,32},{32,64},{64,96},{96,0},{1,33},{33,65},{65,97},{97,1},{2,34}... | collective-permute-start | bytes 786440 | tf_op jit(solution)/shard_map/ppermute | solution.py:232
  43.2 15.0 %collective-permute-start.8 = (bf16[4,2,128,128]{3,2,1,0:T(8,128)(2,1)}, bf16[4,2,128,128]{3,2,1,0:T(8,128)(2,1)S(1)}, u32[]{:S(2)}, u32[]{:S(2)}) collective-permute-start(bf16[4,2,128,128]{3,2,1,0:T(8,128)(2,1)} %split_kv.1), channel_id=1, source_target_pairs={{0,64},{32,96},{64,0},{96,32},{1,65},{33,97},{65,1},{97,33},{2,66}... | collective-permute-start | bytes 786440 | tf_op jit(solution)/shard_map/ppermute | solution.py:232
  44.7 13.5 %collective-permute-start.9 = (bf16[4,2,128,128]{3,2,1,0:T(8,128)(2,1)}, bf16[4,2,128,128]{3,2,1,0:T(8,128)(2,1)S(1)}, u32[]{:S(2)}, u32[]{:S(2)}) collective-permute-start(bf16[4,2,128,128]{3,2,1,0:T(8,128)(2,1)} %split_kv.1), channel_id=1, source_target_pairs={{0,96},{32,0},{64,32},{96,64},{1,97},{33,1},{65,33},{97,65},{2,98}... | collective-permute-start | bytes 786440 | tf_op jit(solution)/shard_map/ppermute | solution.py:232
  46.6 11.9 %collective-permute-start.5 = (bf16[4,2,128,128]{3,2,1,0:T(8,128)(2,1)S(1)}, bf16[4,2,128,128]{3,2,1,0:T(8,128)(2,1)S(1)}, u32[]{:S(2)}, u32[]{:S(2)}) collective-permute-start(bf16[4,2,128,128]{3,2,1,0:T(8,128)(2,1)S(1)} %all-to-all-done.2.refs_2_), channel_id=1, source_target_pairs={{0,4},{2,6},{4,0},{6,2},{1,5},{3,7},{5,1},{7,3},{8,12},{10,14},{12... | collective-permute-start | bytes 786440 | tf_op jit(solution)/shard_map/ppermute | solution.py:232
  48.3 11.7 %collective-permute-start.3 = (bf16[4,2,128,128]{3,2,1,0:T(8,128)(2,1)S(1)}, bf16[4,2,128,128]{3,2,1,0:T(8,128)(2,1)S(1)}, u32[]{:S(2)}, u32[]{:S(2)}) collective-permute-start(bf16[4,2,128,128]{3,2,1,0:T(8,128)(2,1)S(1)} %all-to-all-done.2.refs_2_), channel_id=1, source_target_pairs={{0,2},{2,4},{4,6},{6,0},{1,3},{3,5},{5,7},{7,1},{8,10},{10,12},{12... | collective-permute-start | bytes 786440 | tf_op jit(solution)/shard_map/ppermute | solution.py:232
  58.2 11.9 %collective-permute-start.11 = (bf16[4,2,128,128]{3,2,1,0:T(8,128)(2,1)S(1)}, bf16[4,2,128,128]{3,2,1,0:T(8,128)(2,1)S(1)}, u32[]{:S(2)}, u32[]{:S(2)}) collective-permute-start(bf16[4,2,128,128]{3,2,1,0:T(8,128)(2,1)S(1)} %collective-permute-done.8.refs_1_), channel_id=1, source_target_pairs={{0,1},{1,2},{2,3},{3,4},{4,5},{5,6},{6,7},{7,8},{8,9},{9,10},{10,1... | collective-permute-start | bytes 786440 | tf_op jit(solution)/shard_map/ppermute | solution.py:232
  58.5 14.4 %collective-permute-start.12 = (bf16[4,2,128,128]{3,2,1,0:T(8,128)(2,1)S(1)}, bf16[4,2,128,128]{3,2,1,0:T(8,128)(2,1)S(1)}, u32[]{:S(2)}, u32[]{:S(2)}) collective-permute-start(bf16[4,2,128,128]{3,2,1,0:T(8,128)(2,1)S(1)} %collective-permute-done.9.refs_2_), channel_id=1, source_target_pairs={{0,1},{1,2},{2,3},{3,4},{4,5},{5,6},{6,7},{7,8},{8,9},{9,10},{10,1... | collective-permute-start | bytes 786440 | tf_op jit(solution)/shard_map/ppermute | solution.py:232
  60.0 23.2 %collective-permute-start.6 = (bf16[4,2,128,128]{3,2,1,0:T(8,128)(2,1)S(1)}, bf16[4,2,128,128]{3,2,1,0:T(8,128)(2,1)S(1)}, u32[]{:S(2)}, u32[]{:S(2)}) collective-permute-start(bf16[4,2,128,128]{3,2,1,0:T(8,128)(2,1)S(1)} %collective-permute-done.5.refs_2_), channel_id=1, source_target_pairs={{0,1},{1,0},{2,3},{3,2},{4,5},{5,4},{6,7},{7,6},{8,9},{9,8},{10,11... | collective-permute-start | bytes 786440 | tf_op jit(solution)/shard_map/ppermute | solution.py:232
  62.7 26.9 %collective-permute-start.4 = (bf16[4,2,128,128]{3,2,1,0:T(8,128)(2,1)S(1)}, bf16[4,2,128,128]{3,2,1,0:T(8,128)(2,1)}, u32[]{:S(2)}, u32[]{:S(2)}) collective-permute-start(bf16[4,2,128,128]{3,2,1,0:T(8,128)(2,1)S(1)} %collective-permute-done.3.refs_2_), channel_id=1, source_target_pairs={{0,1},{1,0},{2,3},{3,2},{4,5},{5,4},{6,7},{7,6},{8,9},{9,8},{10,11... | collective-permute-start | bytes 786440 | tf_op jit(solution)/shard_map/ppermute | solution.py:232
  67.3 26.6 %collective-permute-start.2 = (bf16[4,2,128,128]{3,2,1,0:T(8,128)(2,1)S(1)}, bf16[4,2,128,128]{3,2,1,0:T(8,128)(2,1)}, u32[]{:S(2)}, u32[]{:S(2)}) collective-permute-start(bf16[4,2,128,128]{3,2,1,0:T(8,128)(2,1)S(1)} %collective-permute-done.1.refs_2_), channel_id=1, source_target_pairs={{0,1},{1,0},{2,3},{3,2},{4,5},{5,4},{6,7},{7,6},{8,9},{9,8},{10,11... | collective-permute-start | bytes 786440 | tf_op jit(solution)/shard_map/ppermute | solution.py:232
  82.7 16.3 %collective-permute-start.24 = (bf16[4,2,128,128]{3,2,1,0:T(8,128)(2,1)}, bf16[4,2,128,128]{3,2,1,0:T(8,128)(2,1)}, u32[]{:S(2)}, u32[]{:S(2)}) collective-permute-start(bf16[4,2,128,128]{3,2,1,0:T(8,128)(2,1)} %get-tuple-element.43), channel_id=1, source_target_pairs={{0,31},{1,0},{2,1},{3,2},{4,3},{5,4},{6,5},{7,6},{8,7},{9,8},{10,9... | collective-permute-start | bytes 786440 | tf_op jit(solution)/shard_map/ppermute | solution.py:232
  82.7 18.5 %collective-permute-start = (bf16[4,2,128,128]{3,2,1,0:T(8,128)(2,1)S(1)}, bf16[4,2,128,128]{3,2,1,0:T(8,128)(2,1)}, u32[]{:S(2)}, u32[]{:S(2)}) collective-permute-start(bf16[4,2,128,128]{3,2,1,0:T(8,128)(2,1)S(1)} %all-to-all-done.2.refs_2_), channel_id=1, source_target_pairs={{0,1},{1,0},{2,3},{3,2},{4,5},{5,4},{6,7},{7,6},{8,9},{9,8},{10,11... | collective-permute-start | bytes 786440 | tf_op jit(solution)/shard_map/ppermute | solution.py:232
  98.4 15.8 %collective-permute-start.22 = (bf16[4,2,128,128]{3,2,1,0:T(8,128)(2,1)S(1)}, bf16[4,2,128,128]{3,2,1,0:T(8,128)(2,1)S(1)}, u32[]{:S(2)}, u32[]{:S(2)}) collective-permute-start(bf16[4,2,128,128]{3,2,1,0:T(8,128)(2,1)S(1)} %copy-done.16), channel_id=1, source_target_pairs={{0,31},{1,0},{2,1},{3,2},{4,3},{5,4},{6,5},{7,6},{8,7},{9,8},{10,9... | collective-permute-start | bytes 786440 | tf_op jit(solution)/shard_map/ppermute | solution.py:232
  98.9 20.6 %collective-permute-start.20 = (bf16[4,2,128,128]{3,2,1,0:T(8,128)(2,1)S(1)}, bf16[4,2,128,128]{3,2,1,0:T(8,128)(2,1)}, u32[]{:S(2)}, u32[]{:S(2)}) collective-permute-start(bf16[4,2,128,128]{3,2,1,0:T(8,128)(2,1)S(1)} %copy-done.14), channel_id=1, source_target_pairs={{0,31},{1,0},{2,1},{3,2},{4,3},{5,4},{6,5},{7,6},{8,7},{9,8},{10,9... | collective-permute-start | bytes 786440 | tf_op jit(solution)/shard_map/ppermute | solution.py:232
  108.7 11.9 %collective-permute-start.13 = (bf16[4,2,128,128]{3,2,1,0:T(8,128)(2,1)}, bf16[4,2,128,128]{3,2,1,0:T(8,128)(2,1)}, u32[]{:S(2)}, u32[]{:S(2)}) collective-permute-start(bf16[4,2,128,128]{3,2,1,0:T(8,128)(2,1)} %get-tuple-element.31), channel_id=1, source_target_pairs={{0,1},{1,0},{2,3},{3,2},{4,5},{5,4},{6,7},{7,6},{8,9},{9,8},{10,11... | collective-permute-start | bytes 786440 | tf_op jit(solution)/shard_map/ppermute | solution.py:232
  109.3 15.5 %collective-permute-start.19 = (bf16[4,2,128,128]{3,2,1,0:T(8,128)(2,1)S(1)}, bf16[4,2,128,128]{3,2,1,0:T(8,128)(2,1)}, u32[]{:S(2)}, u32[]{:S(2)}) collective-permute-start(bf16[4,2,128,128]{3,2,1,0:T(8,128)(2,1)S(1)} %add_convert_fusion.4), channel_id=1, source_target_pairs={{0,2},{2,4},{4,6},{6,0},{1,3},{3,5},{5,7},{7,1},{8,10},{10,12},{12... | collective-permute-start | bytes 786440 | tf_op jit(solution)/shard_map/ppermute | solution.py:232
  111.7 15.2 %collective-permute-start.15 = (bf16[4,2,128,128]{3,2,1,0:T(8,128)(2,1)}, bf16[4,2,128,128]{3,2,1,0:T(8,128)(2,1)}, u32[]{:S(2)}, u32[]{:S(2)}) collective-permute-start(bf16[4,2,128,128]{3,2,1,0:T(8,128)(2,1)} %add_convert_fusion.6), channel_id=1, source_target_pairs={{0,6},{2,0},{4,2},{6,4},{1,7},{3,1},{5,3},{7,5},{8,14},{10,8},{12,... | collective-permute-start | bytes 786440 | tf_op jit(solution)/shard_map/ppermute | solution.py:232
  114.2 12.8 %collective-permute-start.17 = (bf16[4,2,128,128]{3,2,1,0:T(8,128)(2,1)}, bf16[4,2,128,128]{3,2,1,0:T(8,128)(2,1)}, u32[]{:S(2)}, u32[]{:S(2)}) collective-permute-start(bf16[4,2,128,128]{3,2,1,0:T(8,128)(2,1)} %add_convert_fusion.5), channel_id=1, source_target_pairs={{0,4},{2,6},{4,0},{6,2},{1,5},{3,7},{5,1},{7,3},{8,12},{10,14},{12... | collective-permute-start | bytes 786440 | tf_op jit(solution)/shard_map/ppermute | solution.py:232
  116.0 13.1 %all-to-all-start.3 = ((bf16[4,512,128]{2,1,0:T(8,128)(2,1)}), bf16[4,512,128]{2,1,0:T(8,128)(2,1)S(1)}, u32[]{:S(2)}, u32[]{:S(2)}) async-start(bf16[4,512,128]{2,1,0:T(8,128)(2,1)} %get-tuple-element.28), calls=%async_computation.3 | async-start | bytes 1048576 | tf_op jit(solution)/shard_map/all_to_all | solution.py:278
  119.5 15.0 %collective-permute-start.25 = (bf16[4,2,128,128]{3,2,1,0:T(8,128)(2,1)}, bf16[4,2,128,128]{3,2,1,0:T(8,128)(2,1)S(1)}, u32[]{:S(2)}, u32[]{:S(2)}) collective-permute-start(bf16[4,2,128,128]{3,2,1,0:T(8,128)(2,1)} %add_convert_fusion), channel_id=1, source_target_pairs={{0,32},{32,64},{64,96},{96,0},{1,33},{33,65},{65,97},{97,1},{2,34}... | collective-permute-start | bytes 786440 | tf_op jit(solution)/shard_map/ppermute | solution.py:232
  120.6 13.9 %collective-permute-start.23 = (bf16[4,2,128,128]{3,2,1,0:T(8,128)(2,1)}, bf16[4,2,128,128]{3,2,1,0:T(8,128)(2,1)S(1)}, u32[]{:S(2)}, u32[]{:S(2)}) collective-permute-start(bf16[4,2,128,128]{3,2,1,0:T(8,128)(2,1)} %add_convert_fusion.1), channel_id=1, source_target_pairs={{0,64},{32,96},{64,0},{96,32},{1,65},{33,97},{65,1},{97,33},{2,66}... | collective-permute-start | bytes 786440 | tf_op jit(solution)/shard_map/ppermute | solution.py:232
  124.8 11.5 %collective-permute-start.21 = (bf16[4,2,128,128]{3,2,1,0:T(8,128)(2,1)S(1)}, bf16[4,2,128,128]{3,2,1,0:T(8,128)(2,1)S(1)}, u32[]{:S(2)}, u32[]{:S(2)}) collective-permute-start(bf16[4,2,128,128]{3,2,1,0:T(8,128)(2,1)S(1)} %add_convert_fusion.2), channel_id=1, source_target_pairs={{0,96},{32,0},{64,32},{96,64},{1,97},{33,1},{65,33},{97,65},{2,98}... | collective-permute-start | bytes 786440 | tf_op jit(solution)/shard_map/ppermute | solution.py:232
  (24 other events, 204.1 us)
